TPU v7x, 32 devices: a whole 2x2x4 slice. The times are simulated.
32 devices in a mesh: section: 4 (over y, core), ep: 8 (over z, x).
Axes of the slice: x: 2, y: 2, z: 4, core: 2. Of those that a mesh axis runs over, the one named last changes fastest.
Arguments:
- rows_in: bfloat16 [4, 64, 7168], P(None, 'ep'), may hold values from -6 to 6
- routes: int32 [4, 4, 64, 2], P('section', None, 'ep'), may hold values from 0 to 3, all different within a row; in each aligned block of 8 rows (0 to 7, 8 to 15, ..., all dimensions but the last counted through in order) at most 4 rows name the same one
- hot_blocks: int32 [4], P('section'), may hold values from 0 to 15
- gains: float32 [4, 7168], P('section'), may hold values from 0.1 to 1.9
- router: bfloat16 [4, 7168, 4], P('section'), may hold values from -0.0625 to 0.0625
- w_gate: bfloat16 [4, 7168, 4096], P('section', None, 'ep'), may hold values from -0.0625 to 0.0625
- w_up: bfloat16 [4, 7168, 4096], P('section', None, 'ep'), may hold values from -0.0625 to 0.0625
- w_down: bfloat16 [4, 4096, 7168], P('section', 'ep'), may hold values from -0.1875 to 0.1875
Outputs:
- section_rows: bfloat16 [4, 4, 64, 7168], P('section', None, 'ep')
- relative_load: float32 [4, 8], P('section', 'ep')
Inputs may be any that keep to these rules, and one draw needn't show every extreme that they name: `routes`: in every layer and micro-batch the 8 rows of one device name each expert at most 4 times.
All inputs are finite; a program needn't handle non-finite values.
Results may differ from a plain program's by a relative error of at most 0.025.
Values may be sent and summed in bfloat16 or wider, within the bound.
A program may use at most 128 MiB of HBM per device.

v0:
```python
import jax
import jax.numpy as jnp
from jax import lax
from jax.sharding import PartitionSpec as P

FFW = 1024
BLK = 256


def shifted(block, axis, distance):
    devices = range(lax.axis_size(axis))
    route = [(i - distance, i) for i in devices if i - distance in devices]
    return lax.ppermute(block, axis, route)


def local(rows_in, routes, hot_blocks, gains, router, w_gate, w_up, w_down):
    section_index = lax.axis_index("section")
    ep_index = lax.axis_index("ep")
    section_count = lax.axis_size("section")
    micro_count = rows_in.shape[0]
    tok_rows = rows_in.shape[1]
    model_width = rows_in.shape[2]
    expert_count = router.shape[2]
    top_count = routes.shape[3]
    capacity = tok_rows // 2
    blocks_per_expert = FFW // BLK
    hot_index = hot_blocks[0]
    owner_index = hot_index // 2
    hot_expert = hot_index // blocks_per_expert
    norm_gain = gains[0]
    router_w = router[0]
    gate_w = w_gate[0]
    up_w = w_up[0]
    down_w = w_down[0]
    expert_ids = lax.iota(jnp.int32, expert_count)
    route_member = (routes[0][..., None] == expert_ids).astype(jnp.float32)
    expert_local = jnp.sum(route_member, axis=(0, 1, 2))
    expert_total = lax.psum(expert_local, "ep")
    own_expert = ep_index // 2
    home_units = jnp.sum(jnp.where(expert_ids == own_expert, expert_total, 0.0))
    own_hot = jnp.sum(jnp.where(expert_ids == hot_expert, expert_local, 0.0))

    def expert_rows(flat_rows):
        gate_value = jnp.dot(flat_rows, gate_w, preferred_element_type=jnp.float32)
        up_value = jnp.dot(flat_rows, up_w, preferred_element_type=jnp.float32)
        activation = (jax.nn.silu(gate_value) * up_value).astype(jnp.bfloat16)
        return jnp.dot(activation, down_w, preferred_element_type=jnp.float32).astype(jnp.bfloat16)

    def apply_layer(layer_input, route_ids):
        rows_float = layer_input.astype(jnp.float32)
        mean_square = jnp.mean(rows_float * rows_float, axis=-1, keepdims=True)
        normed = (rows_float * lax.rsqrt(mean_square + 1e-06) * norm_gain).astype(jnp.bfloat16)
        scores = jax.nn.sigmoid(jnp.dot(normed, router_w, preferred_element_type=jnp.float32))
        member = (route_ids[..., None] == expert_ids).astype(jnp.float32)
        chosen = jnp.sum(member * scores[:, :, None, :], axis=3)
        gate_weights = 2.5 * chosen / jnp.sum(chosen, axis=2, keepdims=True)
        token_gate = jnp.sum(member * gate_weights[..., None], axis=2)
        routed = jnp.sum(member, axis=2)
        slot_rank = jnp.cumsum(routed, axis=1) - routed
        slot_ids = lax.iota(jnp.float32, capacity)
        placement = jnp.swapaxes(routed, 1, 2)[:, :, None, :] * (
            jnp.swapaxes(slot_rank, 1, 2)[:, :, None, :] == slot_ids[None, None, :, None]
        ).astype(jnp.float32)
        packed = jnp.einsum(
            "mect,mtf->emcf",
            placement.astype(jnp.bfloat16),
            normed,
            preferred_element_type=jnp.float32,
        ).astype(jnp.bfloat16)
        packed = packed.reshape(expert_count, micro_count * capacity, model_width)
        send_rows = jnp.repeat(packed, 2, axis=0)
        recv_rows = lax.all_to_all(send_rows, "ep", split_axis=0, concat_axis=0, tiled=True)
        sources = recv_rows.shape[0]
        item_count = recv_rows.shape[1]
        part = expert_rows(recv_rows.reshape(sources * item_count, model_width))
        part = part.reshape(sources, item_count, model_width)
        home_back = lax.all_to_all(part, "ep", split_axis=0, concat_axis=0, tiled=True)
        combined = home_back.astype(jnp.float32).reshape(
            expert_count, 2, micro_count, capacity, model_width
        )
        pair_sum = combined[:, 0] + combined[:, 1]
        weighting = placement * jnp.swapaxes(token_gate, 1, 2)[:, :, None, :]
        routed_sum = jnp.einsum(
            "mect,emcf->mtf", weighting, pair_sum, precision=lax.Precision.HIGHEST
        )
        return (rows_float + routed_sum).astype(jnp.bfloat16)

    route_ids = routes[0]

    def run_step(step, loop_state):
        incoming, outputs = loop_state
        layer_input = jnp.where(section_index == 0, rows_in, incoming)
        next_rows = apply_layer(layer_input, route_ids)
        outputs = jnp.where(section_index == step, next_rows, outputs)
        return (shifted(next_rows, "section", 1), outputs)

    start_state = (jnp.zeros(rows_in.shape, jnp.bfloat16), jnp.zeros(rows_in.shape, jnp.bfloat16))
    outputs = lax.fori_loop(0, section_count, run_step, start_state)[1]
    unit_count = home_units * (2.0 - (owner_index == ep_index).astype(jnp.float32)) + own_hot
    relative = unit_count / float(micro_count * tok_rows * top_count * blocks_per_expert)
    return (outputs[None], relative.reshape(1, 1))


def solution(mesh):
    return jax.shard_map(
        local,
        mesh=mesh,
        in_specs=(
            P(None, "ep", None),
            P("section", None, "ep", None),
            P("section"),
            P("section", None),
            P("section", None, None),
            P("section", None, "ep"),
            P("section", None, "ep"),
            P("section", "ep", None),
        ),
        out_specs=(P("section", None, "ep", None), P("section", "ep")),
        check_vma=False,
    )
```

profile of v0, /device:TPU:1, one launch (start us, length us, event | category | flops | bytes accessed | tf_op | source)
XLA Modules:
  0.0 512.0 jit_solution(4193816347571856883)
XLA Ops:
  1.5 18.7 %psum.7 = f32[4]{0:T(128)S(1)} all-reduce(f32[4]{0:T(128)S(1)} %convert_reduce_fusion), channel_id=1, replica_groups=mesh['section'=4,'ep'=8] {'ep'}, use_global_device_ids=true, to_apply=%region_9.10 | all-reduce | flops 4 | bytes 32 | tf_op jit(solution)/shard_map/psum | solution.py:38
  24.1 486.0 %while.17 = (s32[]{:T(128)}, bf16[4,8,7168]{2,1,0:T(8,128)(2,1)S(1)}, bf16[4,8,7168]{2,1,0:T(8,128)(2,1)S(1)}, pred[]{:T(512)}, bf16[4,8,7168]{2,1,0:T(8,128)(2,...) while((s32[]{:T(128)}, ...), condition=%wide.region_7.8_spmd.clone, body=%wide.region_0.7_spmd.clone.sunk | while | flops 2877921280 | bytes 92975272 | solution.py:98
  29.0 43.1 %all_to_all.24 = bf16[8,16,7168]{2,1,0:T(8,128)(2,1)S(1)} all-to-all(bf16[8,16,7168]{2,1,0:T(8,128)(2,1)S(1)} %bitcast.91), channel_id=1, replica_groups=mesh['section'=4,'ep'=8] {'ep'}, dimensions={0} | all-to-all | bytes 3670016 | tf_op jit(solution)/shard_map/while/body/eval_jaxpr/all_to_all | solution.py:72
  73.2 8.6 %convolution_convert_fusion.3 = bf16[128,7168]{1,0:T(8,128)(2,1)} fusion(bf16[512,7168]{1,0:T(8,128)(2,1)} %get-tuple-element.493, bf16[128,7168]{1,0:T(8,128)(2,1)S(1)} %bitcast.86, bf16[7168,512]{1,0:T(8,128)(2,1)} %get-tuple-element.492, f32[128,512]{1,0:T(8,128)S(1)} %fusion.71), kind=kOutput, calls=%fused_computation.1.clone.1 | convolution fusion | flops 1880358912 | bytes 18612224 | tf_op jit(solution)/shard_map/while/body/eval_jaxpr/dot_general | solution.py:47
  81.9 4.1 all-to-all-start.1
  86.0 40.2 %all-to-all-done.1 = bf16[8,16,7168]{2,1,0:T(8,128)(2,1)S(1)} async-done(((bf16[8,16,7168]{2,1,0:T(8,128)(2,1)}), bf16[8,16,7168]{2,1,0:T(8,128)(2,1)S(1)}, u32[]{:S(2)}, u32[]{:S(2)}) %all-to-all-start.1) | async-done | bytes 1835040 | tf_op jit(solution)/shard_map/while/body/eval_jaxpr/all_to_all | solution.py:77
  126.2 2.4 reshape.91
  128.6 2.5 fusion.72
  131.1 3.7 select_select_fusion.2
  134.8 7.1 %collective-permute-start = (bf16[4,8,7168]{2,1,0:T(8,128)(2,1)S(1)}, bf16[4,8,7168]{2,1,0:T(8,128)(2,1)S(1)}, u32[]{:S(2)}, u32[]{:S(2)}) collective-permute-start(bf16[4,8,7168]{2,1,0:T(8,128)(2,1)S(1)} %get-tuple-element.451), channel_id=1, source_target_pairs={{0,8},{8,16},{16,24},{1,9},{9,17},{17,25},{2,10},{10,18},{18,26},{... | collective-permute-start | bytes 1376264 | tf_op jit(solution)/shard_map/while/body/eval_jaxpr/ppermute | solution.py:13
  141.9 5.4 %collective-permute-done = bf16[4,8,7168]{2,1,0:T(8,128)(2,1)S(1)} collective-permute-done((bf16[4,8,7168]{2,1,0:T(8,128)(2,1)S(1)}, bf16[4,8,7168]{2,1,0:T(8,128)(2,1)S(1)}, u32[]{:S(2)}, u32[]{:S(2)}) %collective-permute-start) | collective-permute-done | bytes 458784 | tf_op jit(solution)/shard_map/while/body/eval_jaxpr/ppermute | solution.py:13
  152.2 42.3 %all_to_all.24 = bf16[8,16,7168]{2,1,0:T(8,128)(2,1)S(1)} all-to-all(bf16[8,16,7168]{2,1,0:T(8,128)(2,1)S(1)} %bitcast.91), channel_id=1, replica_groups=mesh['section'=4,'ep'=8] {'ep'}, dimensions={0} | all-to-all | bytes 3670016 | tf_op jit(solution)/shard_map/while/body/eval_jaxpr/all_to_all | solution.py:72
  195.6 8.6 %convolution_convert_fusion.3 = bf16[128,7168]{1,0:T(8,128)(2,1)} fusion(bf16[512,7168]{1,0:T(8,128)(2,1)} %get-tuple-element.493, bf16[128,7168]{1,0:T(8,128)(2,1)S(1)} %bitcast.86, bf16[7168,512]{1,0:T(8,128)(2,1)} %get-tuple-element.492, f32[128,512]{1,0:T(8,128)S(1)} %fusion.71), kind=kOutput, calls=%fused_computation.1.clone.1 | convolution fusion | flops 1880358912 | bytes 18612224 | tf_op jit(solution)/shard_map/while/body/eval_jaxpr/dot_general | solution.py:47
  204.2 3.6 all-to-all-start.1
  207.8 43.3 %all-to-all-done.1 = bf16[8,16,7168]{2,1,0:T(8,128)(2,1)S(1)} async-done(((bf16[8,16,7168]{2,1,0:T(8,128)(2,1)}), bf16[8,16,7168]{2,1,0:T(8,128)(2,1)S(1)}, u32[]{:S(2)}, u32[]{:S(2)}) %all-to-all-start.1) | async-done | bytes 1835040 | tf_op jit(solution)/shard_map/while/body/eval_jaxpr/all_to_all | solution.py:77
  253.5 2.5 fusion.72
  256.0 3.7 select_select_fusion.2
  261.7 5.4 %collective-permute-done = bf16[4,8,7168]{2,1,0:T(8,128)(2,1)S(1)} collective-permute-done((bf16[4,8,7168]{2,1,0:T(8,128)(2,1)S(1)}, bf16[4,8,7168]{2,1,0:T(8,128)(2,1)S(1)}, u32[]{:S(2)}, u32[]{:S(2)}) %collective-permute-start) | collective-permute-done | bytes 458784 | tf_op jit(solution)/shard_map/while/body/eval_jaxpr/ppermute | solution.py:13
  271.9 44.4 %all_to_all.24 = bf16[8,16,7168]{2,1,0:T(8,128)(2,1)S(1)} all-to-all(bf16[8,16,7168]{2,1,0:T(8,128)(2,1)S(1)} %bitcast.91), channel_id=1, replica_groups=mesh['section'=4,'ep'=8] {'ep'}, dimensions={0} | all-to-all | bytes 3670016 | tf_op jit(solution)/shard_map/while/body/eval_jaxpr/all_to_all | solution.py:72
  317.4 8.6 %convolution_convert_fusion.3 = bf16[128,7168]{1,0:T(8,128)(2,1)} fusion(bf16[512,7168]{1,0:T(8,128)(2,1)} %get-tuple-element.493, bf16[128,7168]{1,0:T(8,128)(2,1)S(1)} %bitcast.86, bf16[7168,512]{1,0:T(8,128)(2,1)} %get-tuple-element.492, f32[128,512]{1,0:T(8,128)S(1)} %fusion.71), kind=kOutput, calls=%fused_computation.1.clone.1 | convolution fusion | flops 1880358912 | bytes 18612224 | tf_op jit(solution)/shard_map/while/body/eval_jaxpr/dot_general | solution.py:47
  326.1 3.6 all-to-all-start.1
  329.7 42.6 %all-to-all-done.1 = bf16[8,16,7168]{2,1,0:T(8,128)(2,1)S(1)} async-done(((bf16[8,16,7168]{2,1,0:T(8,128)(2,1)}), bf16[8,16,7168]{2,1,0:T(8,128)(2,1)S(1)}, u32[]{:S(2)}, u32[]{:S(2)}) %all-to-all-start.1) | async-done | bytes 1835040 | tf_op jit(solution)/shard_map/while/body/eval_jaxpr/all_to_all | solution.py:77
  374.7 2.5 fusion.72
  377.2 3.7 select_select_fusion.2
  382.8 5.4 %collective-permute-done = bf16[4,8,7168]{2,1,0:T(8,128)(2,1)S(1)} collective-permute-done((bf16[4,8,7168]{2,1,0:T(8,128)(2,1)S(1)}, bf16[4,8,7168]{2,1,0:T(8,128)(2,1)S(1)}, u32[]{:S(2)}, u32[]{:S(2)}) %collective-permute-start) | collective-permute-done | bytes 458784 | tf_op jit(solution)/shard_map/while/body/eval_jaxpr/ppermute | solution.py:13
  393.1 45.1 %all_to_all.24 = bf16[8,16,7168]{2,1,0:T(8,128)(2,1)S(1)} all-to-all(bf16[8,16,7168]{2,1,0:T(8,128)(2,1)S(1)} %bitcast.91), channel_id=1, replica_groups=mesh['section'=4,'ep'=8] {'ep'}, dimensions={0} | all-to-all | bytes 3670016 | tf_op jit(solution)/shard_map/while/body/eval_jaxpr/all_to_all | solution.py:72
  439.3 8.6 %convolution_convert_fusion.3 = bf16[128,7168]{1,0:T(8,128)(2,1)} fusion(bf16[512,7168]{1,0:T(8,128)(2,1)} %get-tuple-element.493, bf16[128,7168]{1,0:T(8,128)(2,1)S(1)} %bitcast.86, bf16[7168,512]{1,0:T(8,128)(2,1)} %get-tuple-element.492, f32[128,512]{1,0:T(8,128)S(1)} %fusion.71), kind=kOutput, calls=%fused_computation.1.clone.1 | convolution fusion | flops 1880358912 | bytes 18612224 | tf_op jit(solution)/shard_map/while/body/eval_jaxpr/dot_general | solution.py:47
  447.9 3.6 all-to-all-start.1
  451.5 42.6 %all-to-all-done.1 = bf16[8,16,7168]{2,1,0:T(8,128)(2,1)S(1)} async-done(((bf16[8,16,7168]{2,1,0:T(8,128)(2,1)}), bf16[8,16,7168]{2,1,0:T(8,128)(2,1)S(1)}, u32[]{:S(2)}, u32[]{:S(2)}) %all-to-all-start.1) | async-done | bytes 1835040 | tf_op jit(solution)/shard_map/while/body/eval_jaxpr/all_to_all | solution.py:77
  496.5 2.5 fusion.72
  499.1 3.7 select_select_fusion.2
  504.7 5.4 %collective-permute-done = bf16[4,8,7168]{2,1,0:T(8,128)(2,1)S(1)} collective-permute-done((bf16[4,8,7168]{2,1,0:T(8,128)(2,1)S(1)}, bf16[4,8,7168]{2,1,0:T(8,128)(2,1)S(1)}, u32[]{:S(2)}, u32[]{:S(2)}) %collective-permute-start) | collective-permute-done | bytes 458784 | tf_op jit(solution)/shard_map/while/body/eval_jaxpr/ppermute | solution.py:13
  (90 shorter events, 40.0 us)
Async XLA Ops:
  24.1 3.2 copy-start.2
  28.5 43.7 %copy-start = (bf16[7168,512]{1,0:T(8,128)(2,1)S(1)}, bf16[7168,512]{1,0:T(8,128)(2,1)}, u32[]{:S(2)}) copy-start(bf16[7168,512]{1,0:T(8,128)(2,1)} %get-tuple-element.491) | copy-start | bytes 22020100 | tf_op jit(solution)/shard_map/while
  81.9 44.3 %all-to-all-start.1 = ((bf16[8,16,7168]{2,1,0:T(8,128)(2,1)}), bf16[8,16,7168]{2,1,0:T(8,128)(2,1)S(1)}, u32[]{:S(2)}, u32[]{:S(2)}) async-start(bf16[8,16,7168]{2,1,0:T(8,128)(2,1)} %bitcast.88), calls=%async_computation.1 | async-start | bytes 3670016 | tf_op jit(solution)/shard_map/while/body/eval_jaxpr/all_to_all | solution.py:77
  134.8 12.5 %collective-permute-start = (bf16[4,8,7168]{2,1,0:T(8,128)(2,1)S(1)}, bf16[4,8,7168]{2,1,0:T(8,128)(2,1)S(1)}, u32[]{:S(2)}, u32[]{:S(2)}) collective-permute-start(bf16[4,8,7168]{2,1,0:T(8,128)(2,1)S(1)} %get-tuple-element.451), channel_id=1, source_target_pairs={{0,8},{8,16},{16,24},{1,9},{9,17},{17,25},{2,10},{10,18},{18,26},{... | collective-permute-start | bytes 1376264 | tf_op jit(solution)/shard_map/while/body/eval_jaxpr/ppermute | solution.py:13
  147.3 3.2 copy-start.2
  151.6 42.8 %copy-start = (bf16[7168,512]{1,0:T(8,128)(2,1)S(1)}, bf16[7168,512]{1,0:T(8,128)(2,1)}, u32[]{:S(2)}) copy-start(bf16[7168,512]{1,0:T(8,128)(2,1)} %get-tuple-element.491) | copy-start | bytes 22020100 | tf_op jit(solution)/shard_map/while
  204.2 46.9 %all-to-all-start.1 = ((bf16[8,16,7168]{2,1,0:T(8,128)(2,1)}), bf16[8,16,7168]{2,1,0:T(8,128)(2,1)S(1)}, u32[]{:S(2)}, u32[]{:S(2)}) async-start(bf16[8,16,7168]{2,1,0:T(8,128)(2,1)} %bitcast.88), calls=%async_computation.1 | async-start | bytes 3670016 | tf_op jit(solution)/shard_map/while/body/eval_jaxpr/all_to_all | solution.py:77
  259.8 7.3 %collective-permute-start = (bf16[4,8,7168]{2,1,0:T(8,128)(2,1)S(1)}, bf16[4,8,7168]{2,1,0:T(8,128)(2,1)S(1)}, u32[]{:S(2)}, u32[]{:S(2)}) collective-permute-start(bf16[4,8,7168]{2,1,0:T(8,128)(2,1)S(1)} %get-tuple-element.451), channel_id=1, source_target_pairs={{0,8},{8,16},{16,24},{1,9},{9,17},{17,25},{2,10},{10,18},{18,26},{... | collective-permute-start | bytes 1376264 | tf_op jit(solution)/shard_map/while/body/eval_jaxpr/ppermute | solution.py:13
  267.1 3.2 copy-start.2
  271.4 44.9 %copy-start = (bf16[7168,512]{1,0:T(8,128)(2,1)S(1)}, bf16[7168,512]{1,0:T(8,128)(2,1)}, u32[]{:S(2)}) copy-start(bf16[7168,512]{1,0:T(8,128)(2,1)} %get-tuple-element.491) | copy-start | bytes 22020100 | tf_op jit(solution)/shard_map/while
  326.1 46.2 %all-to-all-start.1 = ((bf16[8,16,7168]{2,1,0:T(8,128)(2,1)}), bf16[8,16,7168]{2,1,0:T(8,128)(2,1)S(1)}, u32[]{:S(2)}, u32[]{:S(2)}) async-start(bf16[8,16,7168]{2,1,0:T(8,128)(2,1)} %bitcast.88), calls=%async_computation.1 | async-start | bytes 3670016 | tf_op jit(solution)/shard_map/while/body/eval_jaxpr/all_to_all | solution.py:77
  380.9 7.3 %collective-permute-start = (bf16[4,8,7168]{2,1,0:T(8,128)(2,1)S(1)}, bf16[4,8,7168]{2,1,0:T(8,128)(2,1)S(1)}, u32[]{:S(2)}, u32[]{:S(2)}) collective-permute-start(bf16[4,8,7168]{2,1,0:T(8,128)(2,1)S(1)} %get-tuple-element.451), channel_id=1, source_target_pairs={{0,8},{8,16},{16,24},{1,9},{9,17},{17,25},{2,10},{10,18},{18,26},{... | collective-permute-start | bytes 1376264 | tf_op jit(solution)/shard_map/while/body/eval_jaxpr/ppermute | solution.py:13
  388.2 3.2 copy-start.2
  392.6 45.6 %copy-start = (bf16[7168,512]{1,0:T(8,128)(2,1)S(1)}, bf16[7168,512]{1,0:T(8,128)(2,1)}, u32[]{:S(2)}) copy-start(bf16[7168,512]{1,0:T(8,128)(2,1)} %get-tuple-element.491) | copy-start | bytes 22020100 | tf_op jit(solution)/shard_map/while
  447.9 46.2 %all-to-all-start.1 = ((bf16[8,16,7168]{2,1,0:T(8,128)(2,1)}), bf16[8,16,7168]{2,1,0:T(8,128)(2,1)S(1)}, u32[]{:S(2)}, u32[]{:S(2)}) async-start(bf16[8,16,7168]{2,1,0:T(8,128)(2,1)} %bitcast.88), calls=%async_computation.1 | async-start | bytes 3670016 | tf_op jit(solution)/shard_map/while/body/eval_jaxpr/all_to_all | solution.py:77
  502.8 7.3 %collective-permute-start = (bf16[4,8,7168]{2,1,0:T(8,128)(2,1)S(1)}, bf16[4,8,7168]{2,1,0:T(8,128)(2,1)S(1)}, u32[]{:S(2)}, u32[]{:S(2)}) collective-permute-start(bf16[4,8,7168]{2,1,0:T(8,128)(2,1)S(1)} %get-tuple-element.451), channel_id=1, source_target_pairs={{0,8},{8,16},{16,24},{1,9},{9,17},{17,25},{2,10},{10,18},{18,26},{... | collective-permute-start | bytes 1376264 | tf_op jit(solution)/shard_map/while/body/eval_jaxpr/ppermute | solution.py:13
  510.1 0.8 copy-start.1
where the time goes:
time: 513 us; the launch traced here: 512 us
  blocking collectives  194 us (38%)
  waiting for transfers between devices  190 us (37%)
  matrix products  64.8 us (13%)
  starting transfers between devices  27.7 us (5%)
  other arithmetic  16.5 us (3%)
  local copies, waits for them, and re-layouts  14.9 us (3%)
    all_to_all x4, blocking collectives, apply_layer(): lax.all_to_all(send_rows, 'ep', split_axis=0, concat_axis=0, tiled=True)  175 us
    all_to_all x4, waiting for transfers between devices, apply_layer(): lax.all_to_all(part, 'ep', split_axis=0, concat_axis=0, tiled=True)  169 us
    dot_general x4, matrix products, expert_rows(): jnp.dot(activation, down_w, preferred_element_type=jnp.float32)  34.6 us
    ppermute x4, waiting for transfers between devices, shifted(): return lax.ppermute(block, axis, route)  21.6 us
    psum x1, blocking collectives, local(): expert_total = lax.psum(expert_local, 'ep')  18.7 us
    all_to_all x4, starting transfers between devices, apply_layer(): lax.all_to_all(part, 'ep', split_axis=0, concat_axis=0, tiled=True)  14.9 us
    dot_general x4, matrix products, apply_layer(): jnp.einsum('mect,emcf->mtf', weighting, pair_sum, precision=lax.Precision...  14.9 us
    ppermute x4, starting transfers between devices, shifted(): return lax.ppermute(block, axis, route)  12.8 us
  transfers between devices with their start and end apart: 8, of which 8 were waited for; matrix products, arithmetic and copies ran while one was open for 0% of the time, Pallas kernels for 0%

commit v1 on v0

--- a/solution.py
+++ b/solution.py
@@ -35,7 +35,17 @@
     expert_ids = lax.iota(jnp.int32, expert_count)
     route_member = (routes[0][..., None] == expert_ids).astype(jnp.float32)
     expert_local = jnp.sum(route_member, axis=(0, 1, 2))
-    expert_total = lax.psum(expert_local, "ep")
+
+    def scan_unit(z, peer_axis):
+        axis_n = jax.lax.axis_size(peer_axis)
+        side_arr = z
+        for it in [
+            [(nth, nth ^ c) for nth in range(axis_n)] for c in (1, 2, 4, 8, 16) if c < axis_n
+        ]:
+            side_arr = side_arr + jax.lax.ppermute(side_arr, peer_axis, perm=it)
+        return side_arr
+
+    expert_total = scan_unit(expert_local, "ep")
     own_expert = ep_index // 2
     home_units = jnp.sum(jnp.where(expert_ids == own_expert, expert_total, 0.0))
     own_hot = jnp.sum(jnp.where(expert_ids == hot_expert, expert_local, 0.0))

time: 513 us -> 505 us (0.984)
  blocking collectives: 194 us -> 177 us
  starting transfers between devices: 27.7 us -> 33.4 us
    psum x1 -> x0, blocking collectives: 18.7 us -> none  [local(): expert_total = lax.psum(expert_local, 'ep')]
    ppermute x0 -> x3, starting transfers between devices: none -> 5.69 us  [scan_unit(): side_arr = side_arr + jax.lax.ppermute(side_arr, peer_axis, perm=it)]
  transfers between devices with their start and end apart: 8 -> 11, of which waited for: 8 -> 10; matrix products, arithmetic and copies ran while one was open for 0% -> 0% of each run, Pallas kernels for 0% -> 0%
where the time goes in v1:
time: 505 us; the launch traced here: 504 us
  waiting for transfers between devices  192 us (38%)
  blocking collectives  177 us (35%)
  matrix products  64.7 us (13%)
  starting transfers between devices  33.4 us (7%)
  other arithmetic  16.6 us (3%)
  local copies, waits for them, and re-layouts  14.9 us (3%)
    all_to_all x4, blocking collectives, apply_layer(): lax.all_to_all(send_rows, 'ep', split_axis=0, concat_axis=0, tiled=True)  177 us
    all_to_all x4, waiting for transfers between devices, apply_layer(): lax.all_to_all(part, 'ep', split_axis=0, concat_axis=0, tiled=True)  169 us
    dot_general x4, matrix products, expert_rows(): jnp.dot(activation, down_w, preferred_element_type=jnp.float32)  34.5 us
    ppermute x4, waiting for transfers between devices, shifted(): return lax.ppermute(block, axis, route)  21.6 us
    all_to_all x4, starting transfers between devices, apply_layer(): lax.all_to_all(part, 'ep', split_axis=0, concat_axis=0, tiled=True)  15 us
    dot_general x4, matrix products, apply_layer(): jnp.einsum('mect,emcf->mtf', weighting, pair_sum, precision=lax.Precision...  14.9 us
    ppermute x4, starting transfers between devices, shifted(): return lax.ppermute(block, axis, route)  12.8 us
    add x4, other arithmetic, apply_layer(): pair_sum = combined[:, 0] + combined[:, 1]  10.1 us
  transfers between devices with their start and end apart: 11, of which 10 were waited for; matrix products, arithmetic and copies ran while one was open for 0% of the time, Pallas kernels for 0%

profile of v1, /device:TPU:1, one launch (start us, length us, event | category | flops | bytes accessed | tf_op | source)
XLA Modules:
  0.0 503.8 jit_solution(15642452969657385796)
XLA Ops:
  13.3 488.6 %while.17 = (s32[]{:T(128)}, bf16[4,8,7168]{2,1,0:T(8,128)(2,1)S(1)}, bf16[4,8,7168]{2,1,0:T(8,128)(2,1)S(1)}, pred[]{:T(512)}, bf16[4,8,7168]{2,1,0:T(8,128)(2,...) while((s32[]{:T(128)}, ...), condition=%wide.region_7.8_spmd.clone, body=%wide.region_0.7_spmd.clone.sunk | while | flops 2877921280 | bytes 92975272 | solution.py:108
  18.2 45.7 %all_to_all.24 = bf16[8,16,7168]{2,1,0:T(8,128)(2,1)S(1)} all-to-all(bf16[8,16,7168]{2,1,0:T(8,128)(2,1)S(1)} %bitcast.91), channel_id=1, replica_groups=mesh['section'=4,'ep'=8] {'ep'}, dimensions={0} | all-to-all | bytes 3670016 | tf_op jit(solution)/shard_map/while/body/eval_jaxpr/all_to_all | solution.py:82
  65.0 8.6 %convolution_convert_fusion.3 = bf16[128,7168]{1,0:T(8,128)(2,1)} fusion(bf16[512,7168]{1,0:T(8,128)(2,1)} %get-tuple-element.495, bf16[128,7168]{1,0:T(8,128)(2,1)S(1)} %bitcast.86, bf16[7168,512]{1,0:T(8,128)(2,1)} %get-tuple-element.494, f32[128,512]{1,0:T(8,128)S(1)} %fusion.71), kind=kOutput, calls=%fused_computation.1.clone.1 | convolution fusion | flops 1880358912 | bytes 18612224 | tf_op jit(solution)/shard_map/while/body/eval_jaxpr/dot_general | solution.py:57
  73.6 4.2 all-to-all-start.1
  77.8 40.2 %all-to-all-done.1 = bf16[8,16,7168]{2,1,0:T(8,128)(2,1)S(1)} async-done(((bf16[8,16,7168]{2,1,0:T(8,128)(2,1)}), bf16[8,16,7168]{2,1,0:T(8,128)(2,1)S(1)}, u32[]{:S(2)}, u32[]{:S(2)}) %all-to-all-start.1) | async-done | bytes 1835040 | tf_op jit(solution)/shard_map/while/body/eval_jaxpr/all_to_all | solution.py:87
  118.1 2.4 reshape.91
  120.4 2.5 fusion.72
  123.0 3.7 select_select_fusion.2
  126.7 7.0 %collective-permute-start = (bf16[4,8,7168]{2,1,0:T(8,128)(2,1)S(1)}, bf16[4,8,7168]{2,1,0:T(8,128)(2,1)S(1)}, u32[]{:S(2)}, u32[]{:S(2)}) collective-permute-start(bf16[4,8,7168]{2,1,0:T(8,128)(2,1)S(1)} %get-tuple-element.453), channel_id=1, source_target_pairs={{0,8},{8,16},{16,24},{1,9},{9,17},{17,25},{2,10},{10,18},{18,26},{... | collective-permute-start | bytes 1376264 | tf_op jit(solution)/shard_map/while/body/eval_jaxpr/ppermute | solution.py:13
  133.7 5.4 %collective-permute-done = bf16[4,8,7168]{2,1,0:T(8,128)(2,1)S(1)} collective-permute-done((bf16[4,8,7168]{2,1,0:T(8,128)(2,1)S(1)}, bf16[4,8,7168]{2,1,0:T(8,128)(2,1)S(1)}, u32[]{:S(2)}, u32[]{:S(2)}) %collective-permute-start) | collective-permute-done | bytes 458784 | tf_op jit(solution)/shard_map/while/body/eval_jaxpr/ppermute | solution.py:13
  143.9 42.3 %all_to_all.24 = bf16[8,16,7168]{2,1,0:T(8,128)(2,1)S(1)} all-to-all(bf16[8,16,7168]{2,1,0:T(8,128)(2,1)S(1)} %bitcast.91), channel_id=1, replica_groups=mesh['section'=4,'ep'=8] {'ep'}, dimensions={0} | all-to-all | bytes 3670016 | tf_op jit(solution)/shard_map/while/body/eval_jaxpr/all_to_all | solution.py:82
  187.4 8.6 %convolution_convert_fusion.3 = bf16[128,7168]{1,0:T(8,128)(2,1)} fusion(bf16[512,7168]{1,0:T(8,128)(2,1)} %get-tuple-element.495, bf16[128,7168]{1,0:T(8,128)(2,1)S(1)} %bitcast.86, bf16[7168,512]{1,0:T(8,128)(2,1)} %get-tuple-element.494, f32[128,512]{1,0:T(8,128)S(1)} %fusion.71), kind=kOutput, calls=%fused_computation.1.clone.1 | convolution fusion | flops 1880358912 | bytes 18612224 | tf_op jit(solution)/shard_map/while/body/eval_jaxpr/dot_general | solution.py:57
  196.0 3.6 all-to-all-start.1
  199.6 43.3 %all-to-all-done.1 = bf16[8,16,7168]{2,1,0:T(8,128)(2,1)S(1)} async-done(((bf16[8,16,7168]{2,1,0:T(8,128)(2,1)}), bf16[8,16,7168]{2,1,0:T(8,128)(2,1)S(1)}, u32[]{:S(2)}, u32[]{:S(2)}) %all-to-all-start.1) | async-done | bytes 1835040 | tf_op jit(solution)/shard_map/while/body/eval_jaxpr/all_to_all | solution.py:87
  243.0 2.4 reshape.91
  245.3 2.5 fusion.72
  247.9 3.7 select_select_fusion.2
  253.5 5.4 %collective-permute-done = bf16[4,8,7168]{2,1,0:T(8,128)(2,1)S(1)} collective-permute-done((bf16[4,8,7168]{2,1,0:T(8,128)(2,1)S(1)}, bf16[4,8,7168]{2,1,0:T(8,128)(2,1)S(1)}, u32[]{:S(2)}, u32[]{:S(2)}) %collective-permute-start) | collective-permute-done | bytes 458784 | tf_op jit(solution)/shard_map/while/body/eval_jaxpr/ppermute | solution.py:13
  263.8 44.4 %all_to_all.24 = bf16[8,16,7168]{2,1,0:T(8,128)(2,1)S(1)} all-to-all(bf16[8,16,7168]{2,1,0:T(8,128)(2,1)S(1)} %bitcast.91), channel_id=1, replica_groups=mesh['section'=4,'ep'=8] {'ep'}, dimensions={0} | all-to-all | bytes 3670016 | tf_op jit(solution)/shard_map/while/body/eval_jaxpr/all_to_all | solution.py:82
  309.3 8.6 %convolution_convert_fusion.3 = bf16[128,7168]{1,0:T(8,128)(2,1)} fusion(bf16[512,7168]{1,0:T(8,128)(2,1)} %get-tuple-element.495, bf16[128,7168]{1,0:T(8,128)(2,1)S(1)} %bitcast.86, bf16[7168,512]{1,0:T(8,128)(2,1)} %get-tuple-element.494, f32[128,512]{1,0:T(8,128)S(1)} %fusion.71), kind=kOutput, calls=%fused_computation.1.clone.1 | convolution fusion | flops 1880358912 | bytes 18612224 | tf_op jit(solution)/shard_map/while/body/eval_jaxpr/dot_general | solution.py:57
  317.9 3.6 all-to-all-start.1
  321.5 42.6 %all-to-all-done.1 = bf16[8,16,7168]{2,1,0:T(8,128)(2,1)S(1)} async-done(((bf16[8,16,7168]{2,1,0:T(8,128)(2,1)}), bf16[8,16,7168]{2,1,0:T(8,128)(2,1)S(1)}, u32[]{:S(2)}, u32[]{:S(2)}) %all-to-all-start.1) | async-done | bytes 1835040 | tf_op jit(solution)/shard_map/while/body/eval_jaxpr/all_to_all | solution.py:87
  366.5 2.5 fusion.72
  369.0 3.7 select_select_fusion.2
  374.7 5.4 %collective-permute-done = bf16[4,8,7168]{2,1,0:T(8,128)(2,1)S(1)} collective-permute-done((bf16[4,8,7168]{2,1,0:T(8,128)(2,1)S(1)}, bf16[4,8,7168]{2,1,0:T(8,128)(2,1)S(1)}, u32[]{:S(2)}, u32[]{:S(2)}) %collective-permute-start) | collective-permute-done | bytes 458784 | tf_op jit(solution)/shard_map/while/body/eval_jaxpr/ppermute | solution.py:13
  384.9 45.1 %all_to_all.24 = bf16[8,16,7168]{2,1,0:T(8,128)(2,1)S(1)} all-to-all(bf16[8,16,7168]{2,1,0:T(8,128)(2,1)S(1)} %bitcast.91), channel_id=1, replica_groups=mesh['section'=4,'ep'=8] {'ep'}, dimensions={0} | all-to-all | bytes 3670016 | tf_op jit(solution)/shard_map/while/body/eval_jaxpr/all_to_all | solution.py:82
  431.1 8.6 %convolution_convert_fusion.3 = bf16[128,7168]{1,0:T(8,128)(2,1)} fusion(bf16[512,7168]{1,0:T(8,128)(2,1)} %get-tuple-element.495, bf16[128,7168]{1,0:T(8,128)(2,1)S(1)} %bitcast.86, bf16[7168,512]{1,0:T(8,128)(2,1)} %get-tuple-element.494, f32[128,512]{1,0:T(8,128)S(1)} %fusion.71), kind=kOutput, calls=%fused_computation.1.clone.1 | convolution fusion | flops 1880358912 | bytes 18612224 | tf_op jit(solution)/shard_map/while/body/eval_jaxpr/dot_general | solution.py:57
  439.8 3.6 all-to-all-start.1
  443.4 42.6 %all-to-all-done.1 = bf16[8,16,7168]{2,1,0:T(8,128)(2,1)S(1)} async-done(((bf16[8,16,7168]{2,1,0:T(8,128)(2,1)}), bf16[8,16,7168]{2,1,0:T(8,128)(2,1)S(1)}, u32[]{:S(2)}, u32[]{:S(2)}) %all-to-all-start.1) | async-done | bytes 1835040 | tf_op jit(solution)/shard_map/while/body/eval_jaxpr/all_to_all | solution.py:87
  488.4 2.5 fusion.72
  490.9 3.7 select_select_fusion.2
  496.5 5.4 %collective-permute-done = bf16[4,8,7168]{2,1,0:T(8,128)(2,1)S(1)} collective-permute-done((bf16[4,8,7168]{2,1,0:T(8,128)(2,1)S(1)}, bf16[4,8,7168]{2,1,0:T(8,128)(2,1)S(1)}, u32[]{:S(2)}, u32[]{:S(2)}) %collective-permute-start) | collective-permute-done | bytes 458784 | tf_op jit(solution)/shard_map/while/body/eval_jaxpr/ppermute | solution.py:13
  (96 shorter events, 45.5 us)
Async XLA Ops:
  1.4 3.4 collective-permute-start.1
  5.5 2.4 collective-permute-start.2
  7.9 3.3 collective-permute-start.3
  13.3 3.2 copy-start.2
  17.7 46.2 %copy-start = (bf16[7168,512]{1,0:T(8,128)(2,1)S(1)}, bf16[7168,512]{1,0:T(8,128)(2,1)}, u32[]{:S(2)}) copy-start(bf16[7168,512]{1,0:T(8,128)(2,1)} %get-tuple-element.493) | copy-start | bytes 22020100 | tf_op jit(solution)/shard_map/while
  73.6 44.4 %all-to-all-start.1 = ((bf16[8,16,7168]{2,1,0:T(8,128)(2,1)}), bf16[8,16,7168]{2,1,0:T(8,128)(2,1)S(1)}, u32[]{:S(2)}, u32[]{:S(2)}) async-start(bf16[8,16,7168]{2,1,0:T(8,128)(2,1)} %bitcast.88), calls=%async_computation.1 | async-start | bytes 3670016 | tf_op jit(solution)/shard_map/while/body/eval_jaxpr/all_to_all | solution.py:87
  126.7 12.4 %collective-permute-start = (bf16[4,8,7168]{2,1,0:T(8,128)(2,1)S(1)}, bf16[4,8,7168]{2,1,0:T(8,128)(2,1)S(1)}, u32[]{:S(2)}, u32[]{:S(2)}) collective-permute-start(bf16[4,8,7168]{2,1,0:T(8,128)(2,1)S(1)} %get-tuple-element.453), channel_id=1, source_target_pairs={{0,8},{8,16},{16,24},{1,9},{9,17},{17,25},{2,10},{10,18},{18,26},{... | collective-permute-start | bytes 1376264 | tf_op jit(solution)/shard_map/while/body/eval_jaxpr/ppermute | solution.py:13
  139.1 3.2 copy-start.2
  143.4 42.8 %copy-start = (bf16[7168,512]{1,0:T(8,128)(2,1)S(1)}, bf16[7168,512]{1,0:T(8,128)(2,1)}, u32[]{:S(2)}) copy-start(bf16[7168,512]{1,0:T(8,128)(2,1)} %get-tuple-element.493) | copy-start | bytes 22020100 | tf_op jit(solution)/shard_map/while
  196.0 46.9 %all-to-all-start.1 = ((bf16[8,16,7168]{2,1,0:T(8,128)(2,1)}), bf16[8,16,7168]{2,1,0:T(8,128)(2,1)S(1)}, u32[]{:S(2)}, u32[]{:S(2)}) async-start(bf16[8,16,7168]{2,1,0:T(8,128)(2,1)} %bitcast.88), calls=%async_computation.1 | async-start | bytes 3670016 | tf_op jit(solution)/shard_map/while/body/eval_jaxpr/all_to_all | solution.py:87
  251.6 7.3 %collective-permute-start = (bf16[4,8,7168]{2,1,0:T(8,128)(2,1)S(1)}, bf16[4,8,7168]{2,1,0:T(8,128)(2,1)S(1)}, u32[]{:S(2)}, u32[]{:S(2)}) collective-permute-start(bf16[4,8,7168]{2,1,0:T(8,128)(2,1)S(1)} %get-tuple-element.453), channel_id=1, source_target_pairs={{0,8},{8,16},{16,24},{1,9},{9,17},{17,25},{2,10},{10,18},{18,26},{... | collective-permute-start | bytes 1376264 | tf_op jit(solution)/shard_map/while/body/eval_jaxpr/ppermute | solution.py:13
  258.9 3.2 copy-start.2
  263.3 44.9 %copy-start = (bf16[7168,512]{1,0:T(8,128)(2,1)S(1)}, bf16[7168,512]{1,0:T(8,128)(2,1)}, u32[]{:S(2)}) copy-start(bf16[7168,512]{1,0:T(8,128)(2,1)} %get-tuple-element.493) | copy-start | bytes 22020100 | tf_op jit(solution)/shard_map/while
  317.9 46.2 %all-to-all-start.1 = ((bf16[8,16,7168]{2,1,0:T(8,128)(2,1)}), bf16[8,16,7168]{2,1,0:T(8,128)(2,1)S(1)}, u32[]{:S(2)}, u32[]{:S(2)}) async-start(bf16[8,16,7168]{2,1,0:T(8,128)(2,1)} %bitcast.88), calls=%async_computation.1 | async-start | bytes 3670016 | tf_op jit(solution)/shard_map/while/body/eval_jaxpr/all_to_all | solution.py:87
  372.7 7.3 %collective-permute-start = (bf16[4,8,7168]{2,1,0:T(8,128)(2,1)S(1)}, bf16[4,8,7168]{2,1,0:T(8,128)(2,1)S(1)}, u32[]{:S(2)}, u32[]{:S(2)}) collective-permute-start(bf16[4,8,7168]{2,1,0:T(8,128)(2,1)S(1)} %get-tuple-element.453), channel_id=1, source_target_pairs={{0,8},{8,16},{16,24},{1,9},{9,17},{17,25},{2,10},{10,18},{18,26},{... | collective-permute-start | bytes 1376264 | tf_op jit(solution)/shard_map/while/body/eval_jaxpr/ppermute | solution.py:13
  380.1 3.2 copy-start.2
  384.4 45.6 %copy-start = (bf16[7168,512]{1,0:T(8,128)(2,1)S(1)}, bf16[7168,512]{1,0:T(8,128)(2,1)}, u32[]{:S(2)}) copy-start(bf16[7168,512]{1,0:T(8,128)(2,1)} %get-tuple-element.493) | copy-start | bytes 22020100 | tf_op jit(solution)/shard_map/while
  439.8 46.2 %all-to-all-start.1 = ((bf16[8,16,7168]{2,1,0:T(8,128)(2,1)}), bf16[8,16,7168]{2,1,0:T(8,128)(2,1)S(1)}, u32[]{:S(2)}, u32[]{:S(2)}) async-start(bf16[8,16,7168]{2,1,0:T(8,128)(2,1)} %bitcast.88), calls=%async_computation.1 | async-start | bytes 3670016 | tf_op jit(solution)/shard_map/while/body/eval_jaxpr/all_to_all | solution.py:87
  494.6 7.3 %collective-permute-start = (bf16[4,8,7168]{2,1,0:T(8,128)(2,1)S(1)}, bf16[4,8,7168]{2,1,0:T(8,128)(2,1)S(1)}, u32[]{:S(2)}, u32[]{:S(2)}) collective-permute-start(bf16[4,8,7168]{2,1,0:T(8,128)(2,1)S(1)} %get-tuple-element.453), channel_id=1, source_target_pairs={{0,8},{8,16},{16,24},{1,9},{9,17},{17,25},{2,10},{10,18},{18,26},{... | collective-permute-start | bytes 1376264 | tf_op jit(solution)/shard_map/while/body/eval_jaxpr/ppermute | solution.py:13
  501.9 0.8 copy-start.1
